TPU v7x, 32 devices: a whole 2x2x4 slice. The times are simulated.
32 devices in a mesh: groups: 2 (over x), hid: 16 (over z, y, core).
Axes of the slice: x: 2, y: 2, z: 4, core: 2. Of those that a mesh axis runs over, the one named last changes fastest.
Arguments:
- tokens: bfloat16 [256, 8192], P(('groups', 'hid')), parts along dimension 0, may hold values from -6 to 6
- norm_gain: float32 [8192], replicated, may hold values from 0.1 to 1.9
- gate_weight: bfloat16 [8192, 16384], P(None, 'hid'), may hold values from -0.0625 to 0.0625
- up_weight: bfloat16 [8192, 16384], P(None, 'hid'), may hold values from -0.0625 to 0.0625
- down_weight: bfloat16 [16384, 8192], P('hid'), may hold values from -0.046875 to 0.046875
- clip_scale: float32 [16384], P('hid'), may hold values from 0.002 to 0.02
Outputs:
- mixed: bfloat16 [256, 8192], P(('groups', 'hid')), parts along dimension 0
There are 2 independent parts, one for each index of `groups`. A program takes and returns all parts, laid end to end along the dimension named above; an argument that names none is the same for every part. Nothing has to cross between parts.
All inputs are finite; a program needn't handle non-finite values.
Results may differ from a plain program's by a relative error of at most 0.006.
Values may be sent and summed in bfloat16 or wider, within the bound.
A program may use at most 128 MiB of HBM per device.

v0:
```python
import functools
import math

import jax
import jax.numpy as jnp
from jax import lax
from jax.experimental import pallas as pl
from jax.experimental.pallas import tpu as pltpu
from jax.sharding import PartitionSpec as P

BLOCK = 256
STEPS = 4
OUT_STEPS = 8
LAG = (1, 4, 7)
TILE = 256
MESH = pl.DeviceIdType.MESH
BF = jnp.bfloat16
F32 = jnp.float32


def walsh(parts):
    parts = list(parts)
    half = 1
    while half < len(parts):
        for at in range(len(parts)):
            if at & half == 0:
                low, high = parts[at], parts[at + half]
                parts[at], parts[at + half] = low + high, low - high
        half *= 2
    return parts


def kernel(n, tok, gain, wg, wu, wd, clip, out,
           pair, x, vg, vu, vd, gate, up, table, hs, hr, bs, br, y,
           cs, cr, own, ys, yr, zs, zr, fs, fr, fk,
           wsem, dsem, pair_sem, ag_send, z_recv, y_recv, c_recv,
           a_send, a_recv, rs_send, rc_recv, ry_recv, rz_recv, rf_recv):
    me = lax.axis_index("hid")
    line = n // 4
    a, b, c = me // 4, (me // 2) % 2, me % 2
    rows, width = tok.shape
    both = 2 * rows
    local = vg.shape[1]
    total = n * rows
    span = width // STEPS
    piece = span // 2
    outs = out.shape[1]
    ospan = outs // OUT_STEPS
    opiece = ospan // 2
    core_peer = me + 1 - 2 * c
    y_peer = (a * 2 + 1 - b) * 2 + c

    def at_line(shift):
        return lax.rem(a + shift, line)

    def device(a_at):
        return (a_at * 2 + b) * 2 + c

    def strip(a_at, b_at):
        return pl.ds(pl.multiple_of((a_at * 2 + b_at) * both, both), both)

    def send(src, dst, ssem, rsem, to):
        pltpu.make_async_remote_copy(
            src_ref=src, dst_ref=dst, send_sem=ssem, recv_sem=rsem,
            device_id={"hid": to}, device_id_type=MESH).start()

    def settle(ref, sem):
        pltpu.make_async_copy(ref, ref, sem).wait()

    weight_copies = []
    for s in range(STEPS):
        part = pl.ds(s * span, span)
        weight_copies.append((
            pltpu.make_async_copy(wg.at[part, :], vg.at[part, :], wsem.at[0, s]),
            pltpu.make_async_copy(wu.at[part, :], vu.at[part, :], wsem.at[1, s])))
        for copy in weight_copies[-1]:
            copy.start()
    down_copies = []
    for t in range(OUT_STEPS):
        part = pl.ds(t * ospan, ospan)
        down_copies.append(pltpu.make_async_copy(wd.at[:, part], vd.at[:, part], dsem.at[t]))
        down_copies[-1].start()

    barrier = pltpu.get_barrier_semaphore()
    for shift in range(1, n):
        pl.semaphore_signal(barrier, inc=1, device_id={"hid": lax.rem(me + shift, n)}, device_id_type=MESH)
    pl.semaphore_wait(barrier, n - 1)

    send(tok, pair, pair_sem.at[0], pair_sem.at[1], core_peer)
    at_row = lax.broadcasted_iota(jnp.int32, (BLOCK, BLOCK), 0)
    at_col = lax.broadcasted_iota(jnp.int32, (BLOCK, BLOCK), 1)
    bits = at_row & at_col
    folded = bits
    for place in range(1, (BLOCK - 1).bit_length()):
        folded = folded ^ (bits >> place)
    table[...] = (1 - 2 * (folded & 1)).astype(F32).astype(BF)

    def normalized(ref):
        values = ref[...].astype(F32)
        inverse = lax.rsqrt(jnp.mean(values * values, axis=-1, keepdims=True) + 1e-05)
        return values * inverse * gain[...]

    mine = normalized(tok)
    settle(pair, pair_sem.at[1])
    other = normalized(pair)
    first = c == 0
    x[strip(a, b), :] = jnp.concatenate(
        [jnp.where(first, mine, other), jnp.where(first, other, mine)], axis=0).astype(BF)

    def cols(s, half):
        return pl.ds(pl.multiple_of(s * span + half * piece, piece), piece)

    for s in range(STEPS):
        block = x.at[strip(a, b), cols(s, c)]
        send(block, block, ag_send, y_recv.at[s, 0], y_peer)
        for shift in range(1, line):
            send(block, block, ag_send, z_recv.at[s, shift], device(at_line(shift)))

    def relay_over(s):
        for shift in range(1, line):
            block = x.at[strip(at_line(line - shift), b), cols(s, c)]
            settle(block, z_recv.at[s, shift])
            send(block, block, ag_send, y_recv.at[s, shift], y_peer)
            send(block, block, ag_send, c_recv.at[s], core_peer)

    def relay_core(s):
        for shift in range(line):
            block = x.at[strip(at_line(line - shift), 1 - b), cols(s, c)]
            settle(block, y_recv.at[s, shift])
            send(block, block, ag_send, c_recv.at[s], core_peer)

    def project(s):
        settle(x.at[pl.ds(0, total - both), cols(s, 1 - c)], c_recv.at[s])
        for copy in weight_copies[s]:
            copy.wait()
        part = pl.ds(s * span, span)

        @pl.loop(0, local // TILE)
        def _(j):
            tile = pl.ds(pl.multiple_of(j * TILE, TILE), TILE)
            for acc, weight in ((gate, vg), (up, vu)):
                term = jnp.dot(x[:, part], weight[part, tile], preferred_element_type=F32)
                acc[:, tile] = term if s == 0 else acc[:, tile] + term

    for s in range(STEPS + 2):
        if s < STEPS:
            relay_over(s)
        if 0 <= s - 1 < STEPS:
            relay_core(s - 1)
        if 0 <= s - 2 < STEPS:
            project(s - 2)

    blocks = []
    for at in range(local // BLOCK):
        tile = pl.ds(at * BLOCK, BLOCK)
        value = gate[:, tile]
        hidden = value / (1.0 + jnp.exp(-value)) * up[:, tile]
        gate[:, tile] = jnp.dot(hidden.astype(BF), table[...], preferred_element_type=F32)
    half = local // 2
    for d in range(n):
        part = pl.ds(d * rows, rows)
        values = gate[part, :]
        turned = walsh([values[:, at * BLOCK:(at + 1) * BLOCK] for at in range(local // BLOCK)])
        values = turned[0] if len(turned) == 1 else jnp.concatenate(turned, axis=1)
        hs[d] = jnp.concatenate([values[:, :half], values[:, half:]], axis=0).astype(BF)

    def exchange(src, dst, at):
        for shift in range(1, n):
            to = lax.rem(me + shift, n)
            send(src.at[to], dst.at[me], a_send.at[at], a_recv.at[at], to)
        dst[me] = src[me]
        settle(dst.at[pl.ds(0, n - 1)], a_recv.at[at])

    exchange(hs, hr, 0)
    factor = 1.0 / math.sqrt(n * local)
    lanes = 128
    for j in range(half // lanes):
        tile = pl.ds(j * lanes, lanes)
        turned = walsh([hr[d, :, tile].astype(F32) for d in range(n)])
        for d in range(n):
            bs[d, :, tile] = (turned[d] * factor).astype(BF)
    exchange(bs, br, 1)

    limit = 127.0 * clip[...]
    for q in range(n // 2):
        pieces = []
        for d in (2 * q, 2 * q + 1):
            values = br[d].astype(F32)
            pieces.append(jnp.concatenate([values[:rows], values[rows:]], axis=1))
        values = jnp.concatenate(pieces, axis=0)
        y[pl.ds(q * both, both), :] = jnp.clip(values, -limit, limit).astype(BF)

    def product(t, half_at, j):
        tile = pl.ds(pl.multiple_of(t * ospan + half_at * opiece + j * TILE, TILE), TILE)
        return jnp.dot(y[...], vd[:, tile], preferred_element_type=F32)

    def down(t):
        down_copies[t].wait()

        @pl.loop(0, opiece // TILE)
        def _(j):
            cs[t, :, pl.ds(pl.multiple_of(j * TILE, TILE), TILE)] = product(t, 1 - c, j).astype(BF)

        send(cs.at[t], cr.at[t], rs_send.at[0], rc_recv.at[t], core_peer)

        @pl.loop(0, opiece // TILE)
        def _(j):
            own[t, :, pl.ds(pl.multiple_of(j * TILE, TILE), TILE)] = product(t, c, j)

    def over_rows(t):
        settle(cr.at[t], rc_recv.at[t])
        for to in range(line):
            part = strip(to, 1 - b)
            ys[t, pl.ds(to * both, both), :] = (own[t, part, :] + cr[t, part, :].astype(F32)).astype(BF)
        send(ys.at[t], yr.at[t], rs_send.at[1], ry_recv.at[t], y_peer)

    def column_sum(t, a_at):
        part = strip(a_at, b)
        landed = yr[t, pl.ds(pl.multiple_of(a_at * both, both), both), :]
        return own[t, part, :] + cr[t, part, :].astype(F32) + landed.astype(F32)

    def over_line(t):
        settle(yr.at[t], ry_recv.at[t])
        for shift in range(1, line):
            zs[t, shift] = column_sum(t, at_line(shift)).astype(BF)
        for shift in range(1, line):
            send(zs.at[t, shift], zr.at[t, shift], rs_send.at[2], rz_recv.at[t], device(at_line(shift)))

    def finish(t):
        settle(zr.at[t, pl.ds(1, line - 1)], rz_recv.at[t])
        values = column_sum(t, a)
        for shift in range(1, line):
            values = values + zr[t, shift].astype(F32)
        fs[t] = jnp.where(first, values[rows:], values[:rows])
        fk[t] = jnp.where(first, values[:rows], values[rows:])
        send(fs.at[t], fr.at[t], rs_send.at[3], rf_recv.at[t], core_peer)

    stages = ((0, down), (LAG[0], over_rows), (LAG[1], over_line), (LAG[2], finish))
    for t in range(OUT_STEPS + LAG[2]):
        for lag, stage in stages:
            if 0 <= t - lag < OUT_STEPS:
                stage(t - lag)
    for t in range(OUT_STEPS):
        settle(fr.at[t], rf_recv.at[t])
        for half_at, sums in ((c, fk), (1 - c, fr)):
            part = pl.ds(pl.multiple_of(t * ospan + half_at * opiece, opiece), opiece)
            out[:, part] = (tok[:, part].astype(F32) + sums[t]).astype(out.dtype)

    settle(tok, pair_sem.at[0])
    settle(x.at[pl.ds(0, total - both), :], ag_send)
    settle(hs.at[pl.ds(0, n - 1)], a_send.at[0])
    settle(bs.at[pl.ds(0, n - 1)], a_send.at[1])
    settle(cs, rs_send.at[0])
    settle(ys, rs_send.at[1])
    settle(zs.at[:, pl.ds(1, line - 1)], rs_send.at[2])
    settle(fs, rs_send.at[3])


def layer(n, tokens, norm_gain, gate_weight, up_weight, down_weight, clip_scale):
    rows, width = tokens.shape
    local = gate_weight.shape[1]
    outs = down_weight.shape[1]
    total, both, line = n * rows, 2 * rows, n // 4
    opiece = outs // OUT_STEPS // 2
    vmem = pl.BlockSpec(memory_space=pltpu.VMEM)
    hbm = pl.BlockSpec(memory_space=pl.ANY)
    dma = pltpu.SemaphoreType.DMA
    swap = pltpu.VMEM((n, both, local // 2), BF)
    return pl.pallas_call(
        functools.partial(kernel, n),
        out_shape=jax.ShapeDtypeStruct((rows, outs), BF),
        in_specs=[vmem, vmem, hbm, hbm, hbm, vmem],
        out_specs=vmem,
        scratch_shapes=[
            pltpu.VMEM((rows, width), BF),
            pltpu.VMEM((total, width), BF),
            pltpu.VMEM((width, local), BF),
            pltpu.VMEM((width, local), BF),
            pltpu.VMEM((local, outs), BF),
            pltpu.VMEM((total, local), F32),
            pltpu.VMEM((total, local), F32),
            pltpu.VMEM((BLOCK, BLOCK), BF),
            swap, swap, swap, swap,
            pltpu.VMEM((total, local), BF),
            pltpu.VMEM((OUT_STEPS, total, opiece), BF),
            pltpu.VMEM((OUT_STEPS, total, opiece), BF),
            pltpu.VMEM((OUT_STEPS, total, opiece), F32),
            pltpu.VMEM((OUT_STEPS, line * both, opiece), BF),
            pltpu.VMEM((OUT_STEPS, line * both, opiece), BF),
            pltpu.VMEM((OUT_STEPS, line, both, opiece), BF),
            pltpu.VMEM((OUT_STEPS, line, both, opiece), BF),
            pltpu.VMEM((OUT_STEPS, rows, opiece), F32),
            pltpu.VMEM((OUT_STEPS, rows, opiece), F32),
            pltpu.VMEM((OUT_STEPS, rows, opiece), F32),
            dma((2, STEPS)), dma((OUT_STEPS,)), dma((2,)), dma(()),
            dma((STEPS, line)), dma((STEPS, line)), dma((STEPS,)),
            dma((2,)), dma((2,)), dma((4,)),
            dma((OUT_STEPS,)), dma((OUT_STEPS,)), dma((OUT_STEPS,)), dma((OUT_STEPS,)),
        ],
        compiler_params=pltpu.CompilerParams(
            collective_id=0, has_side_effects=True, vmem_limit_bytes=67043328),
    )(tokens, norm_gain.reshape(1, -1), gate_weight, up_weight, down_weight, clip_scale.reshape(1, -1))


def solution(mesh):
    in_specs = (
        P(("groups", "hid"), None),
        P(),
        P(None, "hid"),
        P(None, "hid"),
        P("hid", None),
        P("hid"),
    )
    return jax.shard_map(
        functools.partial(layer, mesh.shape["hid"]), mesh=mesh, in_specs=in_specs,
        out_specs=P(("groups", "hid"), None), check_vma=False)
```

profile of v0, /device:TPU:1, one launch (start us, length us, event | category | flops | bytes accessed | tf_op | source)
XLA Modules:
  0.0 68.0 jit_solution(17063066195690502239)
XLA Ops:
  0.0 66.5 %shard_map.64 = bf16[8,8192]{1,0:T(8,128)(2,1)} custom-call(bf16[8,8192]{1,0:T(8,128)(2,1)} %tok.1, f32[1,8192]{1,0:T(1,128)} %bitcast.2, bf16[8192,1024]{1,0:T(8,128)(2,1)} %wg.1, bf16[8192,1024]{1,0:T(8,128)(2,1)} %wu.1, bf16[1024,8192]{1,0:T(8,128)(2,1)} %wd.1, f32[1,1024]{1,0:T(1,128)} %bitcast.3), custom_call_target="tpu_custom_call" | custom-call | tf_op jit(solution)/shard_map/pallas_call | solution.py:269
  66.5 1.6 %copy.8 = bf16[8,8192]{1,0:T(8,128)(2,1)} copy(bf16[8,8192]{1,0:T(8,128)(2,1)} %shard_map.64) | data formatting | bytes 262144
where the time goes:
time: 68.3 us; the launch traced here: 68 us
  Pallas kernels  66.5 us (97%)
  local copies, waits for them, and re-layouts  1.57 us (2%)
    pallas_call x1, Pallas kernels, layer(): pl.pallas_call(functools.partial(kernel, n), out_shape=jax.ShapeDtypeStru...  66.5 us
    unnamed x1, local copies, waits for them, and re-layouts  1.57 us

commit v1 on v0

v1 whole, which is shorter than its diff:
```python
import functools
import math

import jax
import jax.numpy as jnp
from jax import lax
from jax.experimental import pallas as pl
from jax.experimental.pallas import tpu as pltpu
from jax.sharding import PartitionSpec as P

BLOCK = 256
STEPS = 8
OUT_STEPS = 8
AHEAD = 5
LAG = ((2, 10), (8, 13), (10, 15), (16, 18))
MESH = pl.DeviceIdType.MESH
BF = jnp.bfloat16
F32 = jnp.float32


def walsh(parts):
    parts = list(parts)
    half = 1
    while half < len(parts):
        for at in range(len(parts)):
            if at & half == 0:
                low, high = parts[at], parts[at + half]
                parts[at], parts[at + half] = low + high, low - high
        half *= 2
    return parts


def kernel(n, tok, gain, wg, wu, wd, clip, out,
           x, vg, vu, vd, gate, up, table, hs, hr, bs, br, y,
           own, cs, cr, ys, yr, zs, zr, pr,
           wsem, dsem, ag_send, core_send, relay_send, z_recv, y_recv, c_recv,
           a_send, b_send, a_recv, b_recv, rs_send,
           rc_recv, ry_recv, rz_recv, rp_recv):
    me = lax.axis_index("hid")
    line, chips = n // 4, n // 2
    a, b, c = me // 4, (me // 2) % 2, me % 2
    k = me // 2
    odd = a % 2
    mate = a + 1 - 2 * odd
    rows, width = tok.shape
    local = vg.shape[1]
    span = width // STEPS
    ospan = out.shape[1] // OUT_STEPS
    core_peer = me + 1 - 2 * c
    y_peer = (a * 2 + 1 - b) * 2 + c

    def device(a_at):
        return (a_at * 2 + b) * 2 + c

    def other(nth):
        low = nth + (nth >= a).astype(jnp.int32)
        high = line - 1 - nth - ((line - 1 - nth) <= a).astype(jnp.int32)
        return jnp.where(a < line // 2, low, high)

    def outward(a_at):
        return jnp.where(odd == 0, a_at > a, a_at < a)

    def inward(a_at):
        return jnp.where(odd == 0, a_at < a, a_at > a)

    def send(src, dst, ssem, rsem, to):
        pltpu.make_async_remote_copy(
            src_ref=src, dst_ref=dst, send_sem=ssem, recv_sem=rsem,
            device_id={"hid": to}, device_id_type=MESH).start()

    def settle(ref, sem):
        pltpu.make_async_copy(ref, ref, sem).wait()

    barrier = pltpu.get_barrier_semaphore()
    for shift in range(1, n):
        pl.semaphore_signal(barrier, inc=1, device_id={"hid": lax.rem(me + shift, n)}, device_id_type=MESH)

    weight_copies = []
    for s in range(STEPS):
        part = pl.ds(s * span, span)
        weight_copies.append((
            pltpu.make_async_copy(wg.at[part, :], vg.at[part, :], wsem.at[0, s]),
            pltpu.make_async_copy(wu.at[part, :], vu.at[part, :], wsem.at[1, s])))
        for copy in weight_copies[-1]:
            copy.start()
    down_copies = []
    for t in range(OUT_STEPS):
        part = pl.ds(t * ospan, ospan)
        down_copies.append(pltpu.make_async_copy(wd.at[:, part], vd.at[:, part], dsem.at[t]))
        down_copies[-1].start()

    values = tok[...].astype(F32)
    inverse = lax.rsqrt(jnp.mean(values * values, axis=-1, keepdims=True) + 1e-05)
    x[c, k] = (values * inverse * gain[...]).astype(BF)

    at_row = lax.broadcasted_iota(jnp.int32, (BLOCK, BLOCK), 0)
    at_col = lax.broadcasted_iota(jnp.int32, (BLOCK, BLOCK), 1)
    bits = at_row & at_col
    folded = bits
    for place in range(1, (BLOCK - 1).bit_length()):
        folded = folded ^ (bits >> place)
    table[...] = (1 - 2 * (folded & 1)).astype(F32).astype(BF)

    with jax.named_scope("barrier"):
        pl.semaphore_wait(barrier, n - 1)

    def block(a_at, b_at, s):
        return x.at[c, a_at * 2 + b_at, :, pl.ds(s * span, span)]

    def begin_line(s):
        mine = block(a, b, s)
        for step in range(1, line // 2):
            pair = lax.rem(a // 2 + step, line // 2)
            near = 2 * pair + (pair < a // 2).astype(jnp.int32)
            send(mine, mine, ag_send, z_recv.at[s, a], device(near))
        send(mine, mine, ag_send, z_recv.at[s, a], device(mate))

    def begin_rows(s):
        mine = block(a, b, s)
        send(mine, mine, ag_send, y_recv.at[s, a], y_peer)
        send(mine, mine, core_send, c_recv.at[s], core_peer)

    for s in range(STEPS):
        if s < AHEAD:
            begin_line(s)
        begin_rows(s)

    def relay_line(s):
        for nth in range(line - 1):
            src = other(nth)
            got = block(src, b, s)
            settle(got, z_recv.at[s, src])

            @pl.when(inward(src))
            def _():
                send(got, got, relay_send, z_recv.at[s, src], device(mate))
            send(got, got, ag_send, y_recv.at[s, src], y_peer)
            send(got, got, core_send, c_recv.at[s], core_peer)

    def relay_rows(s):
        for nth in range(line):
            src = a if nth == 0 else other(nth - 1)
            got = block(src, 1 - b, s)
            settle(got, y_recv.at[s, src])
            send(got, got, core_send, c_recv.at[s], core_peer)

    def project(s):
        part = pl.ds(s * span, span)
        with jax.named_scope("pwait"):
            settle(x.at[1 - c, :, :, part], c_recv.at[s])
        with jax.named_scope("wwait"):
            for copy in weight_copies[s]:
                copy.wait()
        left = x[:, :, :, part].reshape(n * rows, span)
        for acc, weight in ((gate, vg), (up, vu)):
            term = jnp.dot(left, weight[part, :], preferred_element_type=F32)
            acc[...] = term if s == 0 else acc[...] + term

    for s in range(STEPS + 3):
        if s < STEPS:
            with jax.named_scope(f"relay_line{s}"):
                relay_line(s)
        if s + AHEAD < STEPS:
            begin_line(s + AHEAD)
        if 0 <= s - 2 < STEPS:
            with jax.named_scope(f"relay_rows{s-2}"):
                relay_rows(s - 2)
        if 0 <= s - 3 < STEPS:
            with jax.named_scope(f"project{s-3}"):
                project(s - 3)

    with jax.named_scope("swiglu"):
        for at in range(local // BLOCK):
            tile = pl.ds(at * BLOCK, BLOCK)
            value = gate[:, tile]
            hidden = value / (1.0 + jnp.exp(-value)) * up[:, tile]
            gate[:, tile] = jnp.dot(hidden.astype(BF), table[...], preferred_element_type=F32)
    with jax.named_scope("walsh0"):
        for h in range(2):
            for q in range(chips):
                values = gate[pl.ds((h * chips + q) * rows, rows), :]
                turned = walsh([values[:, at * BLOCK:(at + 1) * BLOCK] for at in range(local // BLOCK)])
                hs[h, q] = (turned[0] if len(turned) == 1 else jnp.concatenate(turned, axis=1)).astype(BF)

    with jax.named_scope("exch0"):
        send(hs.at[1 - c, k], hr.at[me], a_send, a_recv, core_peer)
        for h in range(2):
            for shift in range(1, chips):
                q = lax.rem(k + shift, chips)
                send(hs.at[h, q], hr.at[me], a_send, a_recv, q * 2 + h)
        keep = pltpu.make_async_copy(hs.at[c, k], hr.at[me], a_recv)
        keep.start()
        settle(hr, a_recv)
    factor = 1.0 / math.sqrt(n * local)
    lanes = 128
    with jax.named_scope("walsh1"):
        for j in range(local // lanes):
            tile = pl.ds(j * lanes, lanes)
            turned = walsh([hr[d, :, tile].astype(F32) for d in range(n)])
            for d in range(n):
                bs[d, :, tile] = (turned[d] * factor).astype(BF)
    with jax.named_scope("exch1"):
        for shift in range(1, n):
            to = lax.rem(me + shift, n)
            send(bs.at[to], br.at[c, k], b_send, b_recv.at[c], to)
        pltpu.make_async_copy(bs.at[me], br.at[c, k], b_recv.at[c]).start()

    limit = 127.0 * clip[...]

    def clipped(h):
        with jax.named_scope(f"cwait{h}"):
            settle(br.at[h], b_recv.at[h])
        for q in range(chips // 2):
            values = jnp.concatenate([br[h, 2 * q].astype(F32), br[h, 2 * q + 1].astype(F32)], axis=0)
            y[h, pl.ds(2 * q * rows, 2 * rows), :] = jnp.clip(values, -limit, limit).astype(BF)

    def down(h, t):
        part = pl.ds(pl.multiple_of(t * ospan, ospan), ospan)
        if h == 0:
            pltpu.make_async_copy(wd.at[:, part], vd.at[:, part], dsem.at[t]).wait()
        own[h, t] = jnp.dot(y[h], vd[:, part], preferred_element_type=F32).reshape(chips, rows, ospan)

        @pl.when(c != h)
        def _():
            cs[t] = own[h, t].astype(BF)
            send(cs.at[t], cr.at[t], rs_send.at[0], rc_recv.at[t], core_peer)

    def over_rows(t):
        settle(cr.at[t], rc_recv.at[t])
        for at in range(line):
            ys[t, at] = (own[c, t, at * 2 + 1 - b] + cr[t, at * 2 + 1 - b].astype(F32)).astype(BF)
        send(ys.at[t], yr.at[t], rs_send.at[1], ry_recv.at[t], y_peer)

    def column(t, at):
        return own[c, t, at * 2 + b] + cr[t, at * 2 + b].astype(F32) + yr[t, at].astype(F32)

    def to_mate(t):
        settle(yr.at[t], ry_recv.at[t])
        for at in range(line):
            @pl.when(outward(at))
            def _():
                zs[t, at] = column(t, at).astype(BF)
                send(zs.at[t, at], zr.at[t, at], rs_send.at[2], rz_recv.at[t, at], device(mate))

    def to_line(t):
        for at in range(line):
            @pl.when(inward(at))
            def _():
                settle(zr.at[t, at], rz_recv.at[t, at])
                zs[t, at] = (column(t, at) + zr[t, at].astype(F32)).astype(BF)
                send(zs.at[t, at], pr.at[t, a // 2], rs_send.at[2], rp_recv.at[t, a // 2], device(at))

    def finish(t):
        settle(zr.at[t, a], rz_recv.at[t, a])
        values = column(t, a) + zr[t, a].astype(F32)
        for step in range(1, line // 2):
            pair = lax.rem(a // 2 + step, line // 2)
            settle(pr.at[t, pair], rp_recv.at[t, pair])
            values = values + pr[t, pair].astype(F32)
        part = pl.ds(pl.multiple_of(t * ospan, ospan), ospan)
        out[:, part] = (tok[:, part].astype(F32) + values).astype(out.dtype)

    def stages(u):
        for (first, last), stage in zip(LAG, (over_rows, to_mate, to_line, finish)):
            t = u - first - (last - first) * c

            @pl.when((t >= 0) & (t < OUT_STEPS))
            def _():
                with jax.named_scope(stage.__name__):
                    stage(t)

    def run(h, start, count):
        @pl.loop(0, count)
        def _(i):
            if h is not None:
                with jax.named_scope("down"):
                    down(h, i)
            stages(start + i)

    clipped(0)
    run(0, 0, OUT_STEPS)
    clipped(1)
    run(1, OUT_STEPS, OUT_STEPS)
    run(None, 2 * OUT_STEPS, LAG[-1][1] - OUT_STEPS)

    with jax.named_scope("drain"):
        for copies in range(1, line):
            @pl.when(jnp.where(odd == 0, a, line - 1 - a) == copies)
            def _():
                settle(x.at[0, pl.ds(0, copies)], relay_send)
        settle(x.at[0], core_send)
        settle(x.at[0, pl.ds(0, line + line // 2)], ag_send)
        settle(hr.at[pl.ds(0, n - 1)], a_send)
        settle(hr.at[pl.ds(0, n - 1)], b_send)
        settle(cs, rs_send.at[0])
        settle(ys, rs_send.at[1])
        settle(zs.at[:, pl.ds(0, line - 1)], rs_send.at[2])


def layer(n, tokens, norm_gain, gate_weight, up_weight, down_weight, clip_scale):
    rows, width = tokens.shape
    local = gate_weight.shape[1]
    outs = down_weight.shape[1]
    line, chips = n // 4, n // 2
    total = n * rows
    ospan = outs // OUT_STEPS
    vmem = pl.BlockSpec(memory_space=pltpu.VMEM)
    hbm = pl.BlockSpec(memory_space=pl.ANY)
    dma = pltpu.SemaphoreType.DMA
    return pl.pallas_call(
        functools.partial(kernel, n),
        out_shape=jax.ShapeDtypeStruct((rows, outs), BF),
        in_specs=[vmem, vmem, hbm, hbm, hbm, vmem],
        out_specs=vmem,
        scratch_shapes=[
            pltpu.VMEM((2, chips, rows, width), BF),
            pltpu.VMEM((width, local), BF),
            pltpu.VMEM((width, local), BF),
            pltpu.VMEM((local, outs), BF),
            pltpu.VMEM((total, local), F32),
            pltpu.VMEM((total, local), F32),
            pltpu.VMEM((BLOCK, BLOCK), BF),
            pltpu.VMEM((2, chips, rows, local), BF),
            pltpu.VMEM((n, rows, local), BF),
            pltpu.VMEM((n, rows, local), BF),
            pltpu.VMEM((2, chips, rows, local), BF),
            pltpu.VMEM((2, chips * rows, local), BF),
            pltpu.VMEM((2, OUT_STEPS, chips, rows, ospan), F32),
            pltpu.VMEM((OUT_STEPS, chips, rows, ospan), BF),
            pltpu.VMEM((OUT_STEPS, chips, rows, ospan), BF),
            pltpu.VMEM((OUT_STEPS, line, rows, ospan), BF),
            pltpu.VMEM((OUT_STEPS, line, rows, ospan), BF),
            pltpu.VMEM((OUT_STEPS, line, rows, ospan), BF),
            pltpu.VMEM((OUT_STEPS, line, rows, ospan), BF),
            pltpu.VMEM((OUT_STEPS, line // 2, rows, ospan), BF),
            dma((2, STEPS)), dma((OUT_STEPS,)), dma(()), dma(()), dma(()),
            dma((STEPS, line)), dma((STEPS, line)), dma((STEPS,)),
            dma(()), dma(()), dma(()), dma((2,)), dma((3,)),
            dma((OUT_STEPS,)), dma((OUT_STEPS,)), dma((OUT_STEPS, line)), dma((OUT_STEPS, line // 2)),
        ],
        compiler_params=pltpu.CompilerParams(
            collective_id=0, has_side_effects=True, vmem_limit_bytes=67043328),
    )(tokens, norm_gain.reshape(1, -1), gate_weight, up_weight, down_weight, clip_scale.reshape(1, -1))


def solution(mesh):
    in_specs = (
        P(("groups", "hid"), None),
        P(),
        P(None, "hid"),
        P(None, "hid"),
        P("hid", None),
        P("hid"),
    )
    return jax.shard_map(
        functools.partial(layer, mesh.shape["hid"]), mesh=mesh, in_specs=in_specs,
        out_specs=P(("groups", "hid"), None), check_vma=False)
```

time: 68.3 us -> 61.3 us (0.90)
  Pallas kernels: 66.5 us -> 59.5 us
    pallas_call x1, Pallas kernels: 66.5 us -> 59.5 us  [layer(): pl.pallas_call(functools.partial(kernel, n), out_shape=jax.ShapeDtypeStru...]
where the time goes in v1:
time: 61.3 us; the launch traced here: 61.1 us
  Pallas kernels  59.5 us (97%)
  local copies, waits for them, and re-layouts  1.57 us (3%)
    pallas_call x1, Pallas kernels, layer(): pl.pallas_call(functools.partial(kernel, n), out_shape=jax.ShapeDtypeStru...  59.5 us
    unnamed x1, local copies, waits for them, and re-layouts  1.57 us

profile of v1, /device:TPU:1, one launch (start us, length us, event | category | flops | bytes accessed | tf_op | source)
XLA Modules:
  0.0 61.1 jit_solution(10421103369416451712)
XLA Ops:
  0.0 59.5 %shard_map.64 = bf16[8,8192]{1,0:T(8,128)(2,1)} custom-call(bf16[8,8192]{1,0:T(8,128)(2,1)} %tok.1, f32[1,8192]{1,0:T(1,128)} %bitcast.2, bf16[8192,1024]{1,0:T(8,128)(2,1)} %wg.1, bf16[8192,1024]{1,0:T(8,128)(2,1)} %wu.1, bf16[1024,8192]{1,0:T(8,128)(2,1)} %wd.1, f32[1,1024]{1,0:T(1,128)} %bitcast.3), custom_call_target="tpu_custom_call" | custom-call | tf_op jit(solution)/shard_map/pallas_call | solution.py:310
  59.5 1.6 %copy.8 = bf16[8,8192]{1,0:T(8,128)(2,1)} copy(bf16[8,8192]{1,0:T(8,128)(2,1)} %shard_map.64) | data formatting | bytes 262144

commit v2 on v1

--- a/solution.py
+++ b/solution.py
@@ -11,8 +11,9 @@
 BLOCK = 256
 STEPS = 8
 OUT_STEPS = 8
-AHEAD = 5
-LAG = ((2, 10), (8, 13), (10, 15), (16, 18))
+AHEAD = 8
+LAG = ((2, 10), (10, 18), (12, 20), (20, 28))
+LATE = 18
 MESH = pl.DeviceIdType.MESH
 BF = jnp.bfloat16
 F32 = jnp.float32
@@ -53,9 +54,9 @@
         return (a_at * 2 + b) * 2 + c
 
     def other(nth):
-        low = nth + (nth >= a).astype(jnp.int32)
-        high = line - 1 - nth - ((line - 1 - nth) <= a).astype(jnp.int32)
-        return jnp.where(a < line // 2, low, high)
+        down = jnp.where(a == 0, 1 + nth, lax.rem(a + line - 1 - nth, line))
+        up = jnp.where(a == line - 1, line - 2 - nth, lax.rem(a + 1 + nth, line))
+        return jnp.where(odd == 0, down, up)
 
     def outward(a_at):
         return jnp.where(odd == 0, a_at > a, a_at < a)
@@ -72,8 +73,17 @@
         pltpu.make_async_copy(ref, ref, sem).wait()
 
     barrier = pltpu.get_barrier_semaphore()
-    for shift in range(1, n):
-        pl.semaphore_signal(barrier, inc=1, device_id={"hid": lax.rem(me + shift, n)}, device_id_type=MESH)
+
+    def greet(to):
+        pl.semaphore_signal(barrier, inc=1, device_id={"hid": to}, device_id_type=MESH)
+
+    greet(core_peer)
+    greet(y_peer)
+    greet(device(mate))
+    for at in range(line):
+        @pl.when(inward(at))
+        def _():
+            greet(device(at))
 
     weight_copies = []
     for s in range(STEPS):
@@ -102,7 +112,7 @@
     table[...] = (1 - 2 * (folded & 1)).astype(F32).astype(BF)
 
     with jax.named_scope("barrier"):
-        pl.semaphore_wait(barrier, n - 1)
+        pl.semaphore_wait(barrier, 2 + line // 2)
 
     def block(a_at, b_at, s):
         return x.at[c, a_at * 2 + b_at, :, pl.ds(s * span, span)]
@@ -125,8 +135,8 @@
             begin_line(s)
         begin_rows(s)
 
-    def relay_line(s):
-        for nth in range(line - 1):
+    def relay_line(s, first, last):
+        for nth in range(first, last):
             src = other(nth)
             got = block(src, b, s)
             settle(got, z_recv.at[s, src])
@@ -156,18 +166,27 @@
             term = jnp.dot(left, weight[part, :], preferred_element_type=F32)
             acc[...] = term if s == 0 else acc[...] + term
 
-    for s in range(STEPS + 3):
+    outer = (a == 0) | (a == line - 1)
+
+    @pl.when(outer)
+    def _():
+        for s in range(STEPS):
+            with jax.named_scope(f"relay_first{s}"):
+                relay_line(s, 0, 1)
+
+    for s in range(STEPS + 5):
         if s < STEPS:
             with jax.named_scope(f"relay_line{s}"):
-                relay_line(s)
-        if s + AHEAD < STEPS:
-            begin_line(s + AHEAD)
-        if 0 <= s - 2 < STEPS:
-            with jax.named_scope(f"relay_rows{s-2}"):
-                relay_rows(s - 2)
-        if 0 <= s - 3 < STEPS:
-            with jax.named_scope(f"project{s-3}"):
-                project(s - 3)
+                @pl.when(jnp.logical_not(outer))
+                def _():
+                    relay_line(s, 0, 1)
+                relay_line(s, 1, line - 1)
+        if 0 <= s - 4 < STEPS:
+            with jax.named_scope(f"relay_rows{s-4}"):
+                relay_rows(s - 4)
+        if 0 <= s - 5 < STEPS:
+            with jax.named_scope(f"project{s-5}"):
+                project(s - 5)
 
     with jax.named_scope("swiglu"):
         for at in range(local // BLOCK):
@@ -227,15 +246,22 @@
 
     def over_rows(t):
         settle(cr.at[t], rc_recv.at[t])
-        for at in range(line):
-            ys[t, at] = (own[c, t, at * 2 + 1 - b] + cr[t, at * 2 + 1 - b].astype(F32)).astype(BF)
-        send(ys.at[t], yr.at[t], rs_send.at[1], ry_recv.at[t], y_peer)
+        for nth in range(line):
+            at = lax.rem(a + nth, line) * 2 + 1 - b
+            ys[t, nth] = (own[c, t, at] + cr[t, at].astype(F32)).astype(BF)
+        far = pl.ds(1, line - 1)
+        send(ys.at[t, far], yr.at[t, far], rs_send.at[1], ry_recv.at[t, 1], y_peer)
+
+    def own_rows():
+        for t in range(OUT_STEPS):
+            send(ys.at[t, 0], yr.at[t, 0], rs_send.at[1], ry_recv.at[t, 0], y_peer)
 
     def column(t, at):
-        return own[c, t, at * 2 + b] + cr[t, at * 2 + b].astype(F32) + yr[t, at].astype(F32)
+        landed = yr[t, lax.rem(at - a + line, line)].astype(F32)
+        return own[c, t, at * 2 + b] + cr[t, at * 2 + b].astype(F32) + landed
 
     def to_mate(t):
-        settle(yr.at[t], ry_recv.at[t])
+        settle(yr.at[t, pl.ds(1, line - 1)], ry_recv.at[t, 1])
         for at in range(line):
             @pl.when(outward(at))
             def _():
@@ -251,6 +277,7 @@
                 send(zs.at[t, at], pr.at[t, a // 2], rs_send.at[2], rp_recv.at[t, a // 2], device(at))
 
     def finish(t):
+        settle(yr.at[t, 0], ry_recv.at[t, 0])
         settle(zr.at[t, a], rz_recv.at[t, a])
         values = column(t, a) + zr[t, a].astype(F32)
         for step in range(1, line // 2):
@@ -261,6 +288,10 @@
         out[:, part] = (tok[:, part].astype(F32) + values).astype(out.dtype)
 
     def stages(u):
+        @pl.when(u == LATE)
+        def _():
+            own_rows()
+
         for (first, last), stage in zip(LAG, (over_rows, to_mate, to_line, finish)):
             t = u - first - (last - first) * c
 
@@ -336,7 +367,7 @@
             dma((2, STEPS)), dma((OUT_STEPS,)), dma(()), dma(()), dma(()),
             dma((STEPS, line)), dma((STEPS, line)), dma((STEPS,)),
             dma(()), dma(()), dma(()), dma((2,)), dma((3,)),
-            dma((OUT_STEPS,)), dma((OUT_STEPS,)), dma((OUT_STEPS, line)), dma((OUT_STEPS, line // 2)),
+            dma((OUT_STEPS,)), dma((OUT_STEPS, 2)), dma((OUT_STEPS, line)), dma((OUT_STEPS, line // 2)),
         ],
         compiler_params=pltpu.CompilerParams(
             collective_id=0, has_side_effects=True, vmem_limit_bytes=67043328),

time: 61.3 us -> 56.7 us (0.925)
  Pallas kernels: 59.5 us -> 55 us
    pallas_call x1, Pallas kernels: 59.5 us -> 55 us  [layer(): pl.pallas_call(functools.partial(kernel, n), out_shape=jax.ShapeDtypeStru...]
where the time goes in v2:
time: 56.7 us; the launch traced here: 56.6 us
  Pallas kernels  55 us (97%)
  local copies, waits for them, and re-layouts  1.57 us (3%)
    pallas_call x1, Pallas kernels, layer(): pl.pallas_call(functools.partial(kernel, n), out_shape=jax.ShapeDtypeStru...  55 us
    unnamed x1, local copies, waits for them, and re-layouts  1.57 us

profile of v2, /device:TPU:1, one launch (start us, length us, event | category | flops | bytes accessed | tf_op | source)
XLA Modules:
  0.0 56.6 jit_solution(6660235636144682386)
XLA Ops:
  0.0 55.0 %shard_map.64 = bf16[8,8192]{1,0:T(8,128)(2,1)} custom-call(bf16[8,8192]{1,0:T(8,128)(2,1)} %tok.1, f32[1,8192]{1,0:T(1,128)} %bitcast.2, bf16[8192,1024]{1,0:T(8,128)(2,1)} %wg.1, bf16[8192,1024]{1,0:T(8,128)(2,1)} %wu.1, bf16[1024,8192]{1,0:T(8,128)(2,1)} %wd.1, f32[1,1024]{1,0:T(1,128)} %bitcast.3), custom_call_target="tpu_custom_call" | custom-call | tf_op jit(solution)/shard_map/pallas_call | solution.py:341
  55.0 1.6 %copy.8 = bf16[8,8192]{1,0:T(8,128)(2,1)} copy(bf16[8,8192]{1,0:T(8,128)(2,1)} %shard_map.64) | data formatting | bytes 262144

commit v3 on v2

--- a/solution.py
+++ b/solution.py
@@ -12,8 +12,9 @@
 STEPS = 8
 OUT_STEPS = 8
 AHEAD = 8
-LAG = ((2, 10), (10, 18), (12, 20), (20, 28))
-LATE = 18
+HEAD = 4
+LAG = ((2, 6), (8, 14), (10, 16), (18, 24))
+LATE = (17, 14)
 MESH = pl.DeviceIdType.MESH
 BF = jnp.bfloat16
 F32 = jnp.float32
@@ -31,10 +32,10 @@
     return parts
 
 
-def kernel(n, tok, gain, wg, wu, wd, clip, out,
-           x, vg, vu, vd, gate, up, table, hs, hr, bs, br, y,
+def kernel(n, tok_in, gain_in, wg, wu, wd, clip_in, out,
+           tok, gain, clip, x, vg, vu, vd, gate, up, table, hs, hr, bs, br, y,
            own, cs, cr, ys, yr, zs, zr, pr,
-           wsem, dsem, ag_send, core_send, relay_send, z_recv, y_recv, c_recv,
+           in_sem, wsem, dsem, ag_send, core_send, relay_send, z_recv, y_recv, c_recv,
            a_send, b_send, a_recv, b_recv, rs_send,
            rc_recv, ry_recv, rz_recv, rp_recv):
     me = lax.axis_index("hid")
@@ -85,6 +86,22 @@
         def _():
             greet(device(at))
 
+    inputs = [pltpu.make_async_copy(src, dst, in_sem.at[at])
+              for at, (src, dst) in enumerate(((tok_in, tok), (gain_in, gain), (clip_in, clip)))]
+    for copy in inputs:
+        copy.start()
+
+    at_row = lax.broadcasted_iota(jnp.int32, (BLOCK, BLOCK), 0)
+    at_col = lax.broadcasted_iota(jnp.int32, (BLOCK, BLOCK), 1)
+    bits = at_row & at_col
+    folded = bits
+    for place in range(1, (BLOCK - 1).bit_length()):
+        folded = folded ^ (bits >> place)
+    table[...] = (1 - 2 * (folded & 1)).astype(F32).astype(BF)
+
+    for copy in inputs:
+        copy.wait()
+
     weight_copies = []
     for s in range(STEPS):
         part = pl.ds(s * span, span)
@@ -103,14 +120,6 @@
     inverse = lax.rsqrt(jnp.mean(values * values, axis=-1, keepdims=True) + 1e-05)
     x[c, k] = (values * inverse * gain[...]).astype(BF)
 
-    at_row = lax.broadcasted_iota(jnp.int32, (BLOCK, BLOCK), 0)
-    at_col = lax.broadcasted_iota(jnp.int32, (BLOCK, BLOCK), 1)
-    bits = at_row & at_col
-    folded = bits
-    for place in range(1, (BLOCK - 1).bit_length()):
-        folded = folded ^ (bits >> place)
-    table[...] = (1 - 2 * (folded & 1)).astype(F32).astype(BF)
-
     with jax.named_scope("barrier"):
         pl.semaphore_wait(barrier, 2 + line // 2)
 
@@ -188,27 +197,32 @@
             with jax.named_scope(f"project{s-5}"):
                 project(s - 5)
 
-    with jax.named_scope("swiglu"):
-        for at in range(local // BLOCK):
-            tile = pl.ds(at * BLOCK, BLOCK)
-            value = gate[:, tile]
-            hidden = value / (1.0 + jnp.exp(-value)) * up[:, tile]
-            gate[:, tile] = jnp.dot(hidden.astype(BF), table[...], preferred_element_type=F32)
-    with jax.named_scope("walsh0"):
-        for h in range(2):
+    half = chips * rows
+    for h in range(2):
+        with jax.named_scope(f"swiglu{h}"):
+            group = pl.ds(h * half, half)
+            for at in range(local // BLOCK):
+                tile = pl.ds(at * BLOCK, BLOCK)
+                value = gate[group, tile]
+                hidden = value / (1.0 + jnp.exp(-value)) * up[group, tile]
+                gate[group, tile] = jnp.dot(hidden.astype(BF), table[...], preferred_element_type=F32)
             for q in range(chips):
                 values = gate[pl.ds((h * chips + q) * rows, rows), :]
                 turned = walsh([values[:, at * BLOCK:(at + 1) * BLOCK] for at in range(local // BLOCK)])
                 hs[h, q] = (turned[0] if len(turned) == 1 else jnp.concatenate(turned, axis=1)).astype(BF)
-
-    with jax.named_scope("exch0"):
-        send(hs.at[1 - c, k], hr.at[me], a_send, a_recv, core_peer)
-        for h in range(2):
             for shift in range(1, chips):
                 q = lax.rem(k + shift, chips)
                 send(hs.at[h, q], hr.at[me], a_send, a_recv, q * 2 + h)
-        keep = pltpu.make_async_copy(hs.at[c, k], hr.at[me], a_recv)
-        keep.start()
+
+            @pl.when(c == h)
+            def _():
+                pltpu.make_async_copy(hs.at[h, k], hr.at[me], a_recv).start()
+
+            @pl.when(c != h)
+            def _():
+                send(hs.at[h, k], hr.at[me], a_send, a_recv, core_peer)
+
+    with jax.named_scope("exch0"):
         settle(hr, a_recv)
     factor = 1.0 / math.sqrt(n * local)
     lanes = 128
@@ -233,16 +247,25 @@
             values = jnp.concatenate([br[h, 2 * q].astype(F32), br[h, 2 * q + 1].astype(F32)], axis=0)
             y[h, pl.ds(2 * q * rows, 2 * rows), :] = jnp.clip(values, -limit, limit).astype(BF)
 
-    def down(h, t):
+    def down(hs_, t):
         part = pl.ds(pl.multiple_of(t * ospan, ospan), ospan)
-        if h == 0:
+        if 0 in hs_:
             pltpu.make_async_copy(wd.at[:, part], vd.at[:, part], dsem.at[t]).wait()
-        own[h, t] = jnp.dot(y[h], vd[:, part], preferred_element_type=F32).reshape(chips, rows, ospan)
-
-        @pl.when(c != h)
-        def _():
-            cs[t] = own[h, t].astype(BF)
+        left = y[hs_[0]] if len(hs_) == 1 else y[...].reshape(2 * half, local)
+        result = jnp.dot(left, vd[:, part], preferred_element_type=F32)
+        if len(hs_) == 1:
+            own[hs_[0], t] = result.reshape(chips, rows, ospan)
+        else:
+            own[:, t] = result.reshape(2, chips, rows, ospan)
+
+        def share():
+            cs[t] = own[1 - c, t].astype(BF)
             send(cs.at[t], cr.at[t], rs_send.at[0], rc_recv.at[t], core_peer)
+
+        if len(hs_) == 1:
+            pl.when(c != hs_[0])(share)
+        else:
+            share()
 
     def over_rows(t):
         settle(cr.at[t], rc_recv.at[t])
@@ -288,7 +311,7 @@
         out[:, part] = (tok[:, part].astype(F32) + values).astype(out.dtype)
 
     def stages(u):
-        @pl.when(u == LATE)
+        @pl.when(u == LATE[0] + (LATE[1] - LATE[0]) * c)
         def _():
             own_rows()
 
@@ -298,21 +321,22 @@
             @pl.when((t >= 0) & (t < OUT_STEPS))
             def _():
                 with jax.named_scope(stage.__name__):
-                    stage(t)
-
-    def run(h, start, count):
+                    stage(lax.rem(t + HEAD * c, OUT_STEPS))
+
+    def run(hs_, start, count, base=0):
         @pl.loop(0, count)
         def _(i):
-            if h is not None:
+            if hs_:
                 with jax.named_scope("down"):
-                    down(h, i)
+                    down(hs_, base + i)
             stages(start + i)
 
     clipped(0)
-    run(0, 0, OUT_STEPS)
+    run((0,), 0, HEAD)
     clipped(1)
-    run(1, OUT_STEPS, OUT_STEPS)
-    run(None, 2 * OUT_STEPS, LAG[-1][1] - OUT_STEPS)
+    run((0, 1), HEAD, OUT_STEPS - HEAD, HEAD)
+    run((1,), OUT_STEPS, HEAD)
+    run((), OUT_STEPS + HEAD, LAG[-1][1] - HEAD)
 
     with jax.named_scope("drain"):
         for copies in range(1, line):
@@ -340,10 +364,13 @@
     dma = pltpu.SemaphoreType.DMA
     return pl.pallas_call(
         functools.partial(kernel, n),
-        out_shape=jax.ShapeDtypeStruct((rows, outs), BF),
-        in_specs=[vmem, vmem, hbm, hbm, hbm, vmem],
+        out_shape=pltpu.VMEM((rows, outs), BF),
+        in_specs=[hbm, hbm, hbm, hbm, hbm, hbm],
         out_specs=vmem,
         scratch_shapes=[
+            pltpu.VMEM((rows, width), BF),
+            pltpu.VMEM((1, width), F32),
+            pltpu.VMEM((1, local), F32),
             pltpu.VMEM((2, chips, rows, width), BF),
             pltpu.VMEM((width, local), BF),
             pltpu.VMEM((width, local), BF),
@@ -364,13 +391,13 @@
             pltpu.VMEM((OUT_STEPS, line, rows, ospan), BF),
             pltpu.VMEM((OUT_STEPS, line, rows, ospan), BF),
             pltpu.VMEM((OUT_STEPS, line // 2, rows, ospan), BF),
-            dma((2, STEPS)), dma((OUT_STEPS,)), dma(()), dma(()), dma(()),
+            dma((3,)), dma((2, STEPS)), dma((OUT_STEPS,)), dma(()), dma(()), dma(()),
             dma((STEPS, line)), dma((STEPS, line)), dma((STEPS,)),
             dma(()), dma(()), dma(()), dma((2,)), dma((3,)),
             dma((OUT_STEPS,)), dma((OUT_STEPS, 2)), dma((OUT_STEPS, line)), dma((OUT_STEPS, line // 2)),
         ],
         compiler_params=pltpu.CompilerParams(
-            collective_id=0, has_side_effects=True, vmem_limit_bytes=67043328),
+            collective_id=0, has_side_effects=True, vmem_limit_bytes=65000000),
     )(tokens, norm_gain.reshape(1, -1), gate_weight, up_weight, down_weight, clip_scale.reshape(1, -1))
 
 

time: 56.7 us -> 54.7 us (0.965)
  Pallas kernels: 55 us -> 53.8 us
  local copies, waits for them, and re-layouts: 1.57 us -> 0.66 us
    pallas_call x1, Pallas kernels: 55 us -> 53.8 us  [layer(): pl.pallas_call(functools.partial(kernel, n), out_shape=pltpu.VMEM((rows,...]
    unnamed x1, local copies, waits for them, and re-layouts: 1.57 us -> 0.66 us
where the time goes in v3:
time: 54.7 us; the launch traced here: 54.5 us
  Pallas kernels  53.8 us (98%)
  local copies, waits for them, and re-layouts  0.66 us (1%)
    pallas_call x1, Pallas kernels, layer(): pl.pallas_call(functools.partial(kernel, n), out_shape=pltpu.VMEM((rows,...  53.8 us

profile of v3, /device:TPU:1, one launch (start us, length us, event | category | flops | bytes accessed | tf_op | source)
XLA Modules:
  0.0 54.5 jit_solution(5978211677120335100)
XLA Ops:
  0.0 53.8 %shard_map.64 = bf16[8,8192]{1,0:T(8,128)(2,1)S(1)} custom-call(bf16[8,8192]{1,0:T(8,128)(2,1)} %tok_in.1, f32[1,8192]{1,0:T(1,128)} %bitcast.2, bf16[8192,1024]{1,0:T(8,128)(2,1)} %wg.1, bf16[8192,1024]{1,0:T(8,128)(2,1)} %wu.1, bf16[1024,8192]{1,0:T(8,128)(2,1)} %wd.1, f32[1,1024]{1,0:T(1,128)} %bitcast.3), custom_call_target="tpu_custom_call" | custom-call | tf_op jit(solution)/shard_map/pallas_call | solution.py:365
  53.9 0.7 %copy.8 = bf16[8,8192]{1,0:T(8,128)(2,1)} copy(bf16[8,8192]{1,0:T(8,128)(2,1)S(1)} %shard_map.64) | data formatting | bytes 262144

commit v4 on v3

--- a/solution.py
+++ b/solution.py
@@ -12,8 +12,11 @@
 STEPS = 8
 OUT_STEPS = 8
 AHEAD = 8
+BEHIND = 4
 HEAD = 4
+TURNED = 1
 LAG = ((2, 6), (8, 14), (10, 16), (18, 24))
+TURNED_LAG = ((2, 6), (7, 11), (13, 17), (18, 24))
 LATE = (17, 14)
 MESH = pl.DeviceIdType.MESH
 BF = jnp.bfloat16
@@ -34,10 +37,10 @@
 
 def kernel(n, tok_in, gain_in, wg, wu, wd, clip_in, out,
            tok, gain, clip, x, vg, vu, vd, gate, up, table, hs, hr, bs, br, y,
-           own, cs, cr, ys, yr, zs, zr, pr,
+           own, cs, cr, ys, yr, zs, zr, pr, zs2, zr2, pr2, yo, yi,
            in_sem, wsem, dsem, ag_send, core_send, relay_send, z_recv, y_recv, c_recv,
            a_send, b_send, a_recv, b_recv, rs_send,
-           rc_recv, ry_recv, rz_recv, rp_recv):
+           rc_recv, ry_recv, rz_recv, rp_recv, sz_recv, sp_recv, sy_recv):
     me = lax.axis_index("hid")
     line, chips = n // 4, n // 2
     a, b, c = me // 4, (me // 2) % 2, me % 2
@@ -183,19 +186,30 @@
             with jax.named_scope(f"relay_first{s}"):
                 relay_line(s, 0, 1)
 
-    for s in range(STEPS + 5):
+    inner = jnp.logical_not(outer)
+    for s in range(STEPS + BEHIND + 1):
         if s < STEPS:
             with jax.named_scope(f"relay_line{s}"):
-                @pl.when(jnp.logical_not(outer))
-                def _():
-                    relay_line(s, 0, 1)
-                relay_line(s, 1, line - 1)
-        if 0 <= s - 4 < STEPS:
-            with jax.named_scope(f"relay_rows{s-4}"):
-                relay_rows(s - 4)
-        if 0 <= s - 5 < STEPS:
-            with jax.named_scope(f"project{s-5}"):
-                project(s - 5)
+                if s <= BEHIND:
+                    @pl.when(inner)
+                    def _():
+                        relay_line(s, 0, 1)
+                    relay_line(s, 1, line - 1)
+                else:
+                    @pl.when(outer)
+                    def _():
+                        relay_line(s, 1, line - 1)
+        if s == BEHIND:
+            @pl.when(inner)
+            def _():
+                for later in range(BEHIND + 1, STEPS):
+                    relay_line(later, 0, line - 1)
+        if 0 <= s - BEHIND < STEPS:
+            with jax.named_scope(f"relay_rows{s-BEHIND}"):
+                relay_rows(s - BEHIND)
+        if 0 <= s - BEHIND - 1 < STEPS:
+            with jax.named_scope(f"project{s-BEHIND-1}"):
+                project(s - BEHIND - 1)
 
     half = chips * rows
     for h in range(2):
@@ -267,7 +281,11 @@
         else:
             share()
 
-    def over_rows(t):
+    def order(at):
+        return lax.rem(at + HEAD * c, OUT_STEPS)
+
+    def over_rows(nth_step):
+        t = order(nth_step)
         settle(cr.at[t], rc_recv.at[t])
         for nth in range(line):
             at = lax.rem(a + nth, line) * 2 + 1 - b
@@ -276,14 +294,16 @@
         send(ys.at[t, far], yr.at[t, far], rs_send.at[1], ry_recv.at[t, 1], y_peer)
 
     def own_rows():
-        for t in range(OUT_STEPS):
+        for at in range(TURNED, OUT_STEPS):
+            t = order(at)
             send(ys.at[t, 0], yr.at[t, 0], rs_send.at[1], ry_recv.at[t, 0], y_peer)
 
     def column(t, at):
         landed = yr[t, lax.rem(at - a + line, line)].astype(F32)
         return own[c, t, at * 2 + b] + cr[t, at * 2 + b].astype(F32) + landed
 
-    def to_mate(t):
+    def to_mate(nth_step):
+        t = order(nth_step)
         settle(yr.at[t, pl.ds(1, line - 1)], ry_recv.at[t, 1])
         for at in range(line):
             @pl.when(outward(at))
@@ -291,7 +311,8 @@
                 zs[t, at] = column(t, at).astype(BF)
                 send(zs.at[t, at], zr.at[t, at], rs_send.at[2], rz_recv.at[t, at], device(mate))
 
-    def to_line(t):
+    def to_line(nth_step):
+        t = order(nth_step)
         for at in range(line):
             @pl.when(inward(at))
             def _():
@@ -299,7 +320,8 @@
                 zs[t, at] = (column(t, at) + zr[t, at].astype(F32)).astype(BF)
                 send(zs.at[t, at], pr.at[t, a // 2], rs_send.at[2], rp_recv.at[t, a // 2], device(at))
 
-    def finish(t):
+    def finish(nth_step):
+        t = order(nth_step)
         settle(yr.at[t, 0], ry_recv.at[t, 0])
         settle(zr.at[t, a], rz_recv.at[t, a])
         values = column(t, a) + zr[t, a].astype(F32)
@@ -310,18 +332,66 @@
         part = pl.ds(pl.multiple_of(t * ospan, ospan), ospan)
         out[:, part] = (tok[:, part].astype(F32) + values).astype(out.dtype)
 
+    def turned_mate(i):
+        t = order(i)
+        settle(cr.at[t], rc_recv.at[t])
+        for at in range(line):
+            @pl.when(outward(at))
+            def _():
+                for b_at in range(2):
+                    q = at * 2 + b_at
+                    zs2[i, at, b_at] = (own[c, t, q] + cr[t, q].astype(F32)).astype(BF)
+                send(zs2.at[i, at], zr2.at[i, at], rs_send.at[3], sz_recv.at[i, at], device(mate))
+
+    def turned_line(i):
+        t = order(i)
+        for at in range(line):
+            @pl.when(inward(at))
+            def _():
+                settle(zr2.at[i, at], sz_recv.at[i, at])
+                for b_at in range(2):
+                    q = at * 2 + b_at
+                    zs2[i, at, b_at] = (own[c, t, q] + cr[t, q].astype(F32) + zr2[i, at, b_at].astype(F32)).astype(BF)
+                send(zs2.at[i, at], pr2.at[i, a // 2], rs_send.at[3], sp_recv.at[i, a // 2], device(at))
+
+    def line_sum(i, b_at):
+        t = order(i)
+        q = a * 2 + b_at
+        values = own[c, t, q] + cr[t, q].astype(F32) + zr2[i, a, b_at].astype(F32)
+        for step in range(1, line // 2):
+            pair = lax.rem(a // 2 + step, line // 2)
+            values = values + pr2[i, pair, b_at].astype(F32)
+        return values
+
+    def turned_rows(i):
+        settle(zr2.at[i, a], sz_recv.at[i, a])
+        for step in range(1, line // 2):
+            pair = lax.rem(a // 2 + step, line // 2)
+            settle(pr2.at[i, pair], sp_recv.at[i, pair])
+        yo[i] = line_sum(i, 1 - b).astype(BF)
+        send(yo.at[i], yi.at[i], rs_send.at[4], sy_recv.at[i], y_peer)
+
+    def turned_finish(i):
+        settle(yi.at[i], sy_recv.at[i])
+        part = pl.ds(pl.multiple_of(order(i) * ospan, ospan), ospan)
+        out[:, part] = (tok[:, part].astype(F32) + line_sum(i, b) + yi[i].astype(F32)).astype(out.dtype)
+
+    table_of_stages = (
+        [(lag, stage, 0, TURNED) for lag, stage in zip(TURNED_LAG, (turned_mate, turned_line, turned_rows, turned_finish))]
+        + [(lag, stage, TURNED, OUT_STEPS) for lag, stage in zip(LAG, (over_rows, to_mate, to_line, finish))])
+
     def stages(u):
         @pl.when(u == LATE[0] + (LATE[1] - LATE[0]) * c)
         def _():
             own_rows()
 
-        for (first, last), stage in zip(LAG, (over_rows, to_mate, to_line, finish)):
-            t = u - first - (last - first) * c
-
-            @pl.when((t >= 0) & (t < OUT_STEPS))
+        for (first, last), stage, low, high in table_of_stages:
+            i = u - first - (last - first) * c
+
+            @pl.when((i >= low) & (i < high))
             def _():
                 with jax.named_scope(stage.__name__):
-                    stage(lax.rem(t + HEAD * c, OUT_STEPS))
+                    stage(i)
 
     def run(hs_, start, count, base=0):
         @pl.loop(0, count)
@@ -348,8 +418,10 @@
         settle(hr.at[pl.ds(0, n - 1)], a_send)
         settle(hr.at[pl.ds(0, n - 1)], b_send)
         settle(cs, rs_send.at[0])
-        settle(ys, rs_send.at[1])
-        settle(zs.at[:, pl.ds(0, line - 1)], rs_send.at[2])
+        settle(ys.at[pl.ds(0, OUT_STEPS - TURNED)], rs_send.at[1])
+        settle(zs.at[pl.ds(0, OUT_STEPS - TURNED), pl.ds(0, line - 1)], rs_send.at[2])
+        settle(zs2.at[:, pl.ds(0, line - 1)], rs_send.at[3])
+        settle(yo, rs_send.at[4])
 
 
 def layer(n, tokens, norm_gain, gate_weight, up_weight, down_weight, clip_scale):
@@ -391,13 +463,19 @@
             pltpu.VMEM((OUT_STEPS, line, rows, ospan), BF),
             pltpu.VMEM((OUT_STEPS, line, rows, ospan), BF),
             pltpu.VMEM((OUT_STEPS, line // 2, rows, ospan), BF),
+            pltpu.VMEM((TURNED, line, 2, rows, ospan), BF),
+            pltpu.VMEM((TURNED, line, 2, rows, ospan), BF),
+            pltpu.VMEM((TURNED, line // 2, 2, rows, ospan), BF),
+            pltpu.VMEM((TURNED, rows, ospan), BF),
+            pltpu.VMEM((TURNED, rows, ospan), BF),
             dma((3,)), dma((2, STEPS)), dma((OUT_STEPS,)), dma(()), dma(()), dma(()),
             dma((STEPS, line)), dma((STEPS, line)), dma((STEPS,)),
-            dma(()), dma(()), dma(()), dma((2,)), dma((3,)),
+            dma(()), dma(()), dma(()), dma((2,)), dma((5,)),
             dma((OUT_STEPS,)), dma((OUT_STEPS, 2)), dma((OUT_STEPS, line)), dma((OUT_STEPS, line // 2)),
+            dma((TURNED, line)), dma((TURNED, line // 2)), dma((TURNED,)),
         ],
         compiler_params=pltpu.CompilerParams(
-            collective_id=0, has_side_effects=True, vmem_limit_bytes=65000000),
+            collective_id=0, has_side_effects=True, vmem_limit_bytes=66000000),
     )(tokens, norm_gain.reshape(1, -1), gate_weight, up_weight, down_weight, clip_scale.reshape(1, -1))
 
 

time: 54.7 us -> 53.2 us (0.973)
  Pallas kernels: 53.8 us -> 52.4 us
    pallas_call x1, Pallas kernels: 53.8 us -> 52.4 us  [layer(): pl.pallas_call(functools.partial(kernel, n), out_shape=pltpu.VMEM((rows,...]
where the time goes in v4:
time: 53.2 us; the launch traced here: 53.1 us
  Pallas kernels  52.4 us (98%)
  local copies, waits for them, and re-layouts  0.66 us (1%)
    pallas_call x1, Pallas kernels, layer(): pl.pallas_call(functools.partial(kernel, n), out_shape=pltpu.VMEM((rows,...  52.4 us

profile of v4, /device:TPU:1, one launch (start us, length us, event | category | flops | bytes accessed | tf_op | source)
XLA Modules:
  0.0 53.1 jit_solution(685728056545443443)
XLA Ops:
  0.0 52.4 %shard_map.64 = bf16[8,8192]{1,0:T(8,128)(2,1)S(1)} custom-call(bf16[8,8192]{1,0:T(8,128)(2,1)} %tok_in.1, f32[1,8192]{1,0:T(1,128)} %bitcast.2, bf16[8192,1024]{1,0:T(8,128)(2,1)} %wg.1, bf16[8192,1024]{1,0:T(8,128)(2,1)} %wu.1, bf16[1024,8192]{1,0:T(8,128)(2,1)} %wd.1, f32[1,1024]{1,0:T(1,128)} %bitcast.3), custom_call_target="tpu_custom_call" | custom-call | tf_op jit(solution)/shard_map/pallas_call | solution.py:437
  52.4 0.7 %copy.8 = bf16[8,8192]{1,0:T(8,128)(2,1)} copy(bf16[8,8192]{1,0:T(8,128)(2,1)S(1)} %shard_map.64) | data formatting | bytes 262144

commit v5 on v4

--- a/solution.py
+++ b/solution.py
@@ -39,8 +39,8 @@
            tok, gain, clip, x, vg, vu, vd, gate, up, table, hs, hr, bs, br, y,
            own, cs, cr, ys, yr, zs, zr, pr, zs2, zr2, pr2, yo, yi,
            in_sem, wsem, dsem, ag_send, core_send, relay_send, z_recv, y_recv, c_recv,
-           a_send, b_send, a_recv, b_recv, rs_send,
-           rc_recv, ry_recv, rz_recv, rp_recv, sz_recv, sp_recv, sy_recv):
+           a_send, b_send, a_recv, b_recv, rs_send, sz_recv, sp_recv, sy_recv):
+    rc_recv, rz_recv = c_recv, z_recv
     me = lax.axis_index("hid")
     line, chips = n // 4, n // 2
     a, b, c = me // 4, (me // 2) % 2, me % 2
@@ -109,15 +109,12 @@
     for s in range(STEPS):
         part = pl.ds(s * span, span)
         weight_copies.append((
-            pltpu.make_async_copy(wg.at[part, :], vg.at[part, :], wsem.at[0, s]),
-            pltpu.make_async_copy(wu.at[part, :], vu.at[part, :], wsem.at[1, s])))
+            pltpu.make_async_copy(wg.at[part, :], vg.at[part, :], wsem.at[s]),
+            pltpu.make_async_copy(wu.at[part, :], vu.at[part, :], wsem.at[s])))
         for copy in weight_copies[-1]:
             copy.start()
-    down_copies = []
-    for t in range(OUT_STEPS):
-        part = pl.ds(t * ospan, ospan)
-        down_copies.append(pltpu.make_async_copy(wd.at[:, part], vd.at[:, part], dsem.at[t]))
-        down_copies[-1].start()
+    pltpu.make_async_copy(wd, vd, dsem).start()
+
 
     values = tok[...].astype(F32)
     inverse = lax.rsqrt(jnp.mean(values * values, axis=-1, keepdims=True) + 1e-05)
@@ -171,8 +168,7 @@
         with jax.named_scope("pwait"):
             settle(x.at[1 - c, :, :, part], c_recv.at[s])
         with jax.named_scope("wwait"):
-            for copy in weight_copies[s]:
-                copy.wait()
+            settle(vg.at[pl.ds(0, 2 * span), :], wsem.at[s])
         left = x[:, :, :, part].reshape(n * rows, span)
         for acc, weight in ((gate, vg), (up, vu)):
             term = jnp.dot(left, weight[part, :], preferred_element_type=F32)
@@ -263,8 +259,6 @@
 
     def down(hs_, t):
         part = pl.ds(pl.multiple_of(t * ospan, ospan), ospan)
-        if 0 in hs_:
-            pltpu.make_async_copy(wd.at[:, part], vd.at[:, part], dsem.at[t]).wait()
         left = y[hs_[0]] if len(hs_) == 1 else y[...].reshape(2 * half, local)
         result = jnp.dot(left, vd[:, part], preferred_element_type=F32)
         if len(hs_) == 1:
@@ -291,12 +285,12 @@
             at = lax.rem(a + nth, line) * 2 + 1 - b
             ys[t, nth] = (own[c, t, at] + cr[t, at].astype(F32)).astype(BF)
         far = pl.ds(1, line - 1)
-        send(ys.at[t, far], yr.at[t, far], rs_send.at[1], ry_recv.at[t, 1], y_peer)
+        send(ys.at[t, far], yr.at[t, far], rs_send.at[1], y_recv.at[t, 1], y_peer)
 
     def own_rows():
         for at in range(TURNED, OUT_STEPS):
             t = order(at)
-            send(ys.at[t, 0], yr.at[t, 0], rs_send.at[1], ry_recv.at[t, 0], y_peer)
+            send(ys.at[t, 0], yr.at[t, 0], rs_send.at[1], y_recv.at[t, 0], y_peer)
 
     def column(t, at):
         landed = yr[t, lax.rem(at - a + line, line)].astype(F32)
@@ -304,7 +298,7 @@
 
     def to_mate(nth_step):
         t = order(nth_step)
-        settle(yr.at[t, pl.ds(1, line - 1)], ry_recv.at[t, 1])
+        settle(yr.at[t, pl.ds(1, line - 1)], y_recv.at[t, 1])
         for at in range(line):
             @pl.when(outward(at))
             def _():
@@ -318,16 +312,16 @@
             def _():
                 settle(zr.at[t, at], rz_recv.at[t, at])
                 zs[t, at] = (column(t, at) + zr[t, at].astype(F32)).astype(BF)
-                send(zs.at[t, at], pr.at[t, a // 2], rs_send.at[2], rp_recv.at[t, a // 2], device(at))
+                send(zs.at[t, at], pr.at[t, a // 2], rs_send.at[2], y_recv.at[t, 2 + a // 2], device(at))
 
     def finish(nth_step):
         t = order(nth_step)
-        settle(yr.at[t, 0], ry_recv.at[t, 0])
+        settle(yr.at[t, 0], y_recv.at[t, 0])
         settle(zr.at[t, a], rz_recv.at[t, a])
         values = column(t, a) + zr[t, a].astype(F32)
         for step in range(1, line // 2):
             pair = lax.rem(a // 2 + step, line // 2)
-            settle(pr.at[t, pair], rp_recv.at[t, pair])
+            settle(pr.at[t, pair], y_recv.at[t, 2 + pair])
             values = values + pr[t, pair].astype(F32)
         part = pl.ds(pl.multiple_of(t * ospan, ospan), ospan)
         out[:, part] = (tok[:, part].astype(F32) + values).astype(out.dtype)
@@ -402,6 +396,7 @@
             stages(start + i)
 
     clipped(0)
+    pltpu.make_async_copy(wd, vd, dsem).wait()
     run((0,), 0, HEAD)
     clipped(1)
     run((0, 1), HEAD, OUT_STEPS - HEAD, HEAD)
@@ -431,6 +426,7 @@
     line, chips = n // 4, n // 2
     total = n * rows
     ospan = outs // OUT_STEPS
+    steps = max(STEPS, OUT_STEPS)
     vmem = pl.BlockSpec(memory_space=pltpu.VMEM)
     hbm = pl.BlockSpec(memory_space=pl.ANY)
     dma = pltpu.SemaphoreType.DMA
@@ -468,10 +464,9 @@
             pltpu.VMEM((TURNED, line // 2, 2, rows, ospan), BF),
             pltpu.VMEM((TURNED, rows, ospan), BF),
             pltpu.VMEM((TURNED, rows, ospan), BF),
-            dma((3,)), dma((2, STEPS)), dma((OUT_STEPS,)), dma(()), dma(()), dma(()),
-            dma((STEPS, line)), dma((STEPS, line)), dma((STEPS,)),
+            dma((3,)), dma((STEPS,)), dma(()), dma(()), dma(()), dma(()),
+            dma((steps, line)), dma((steps, line)), dma((steps,)),
             dma(()), dma(()), dma(()), dma((2,)), dma((5,)),
-            dma((OUT_STEPS,)), dma((OUT_STEPS, 2)), dma((OUT_STEPS, line)), dma((OUT_STEPS, line // 2)),
             dma((TURNED, line)), dma((TURNED, line // 2)), dma((TURNED,)),
         ],
         compiler_params=pltpu.CompilerParams(

time: 53.2 us -> 52.5 us (0.987)
  Pallas kernels: 52.4 us -> 51.7 us
    pallas_call x1, Pallas kernels: 52.4 us -> 51.7 us  [layer(): pl.pallas_call(functools.partial(kernel, n), out_shape=pltpu.VMEM((rows,...]
where the time goes in v5:
time: 52.5 us; the launch traced here: 52.3 us
  Pallas kernels  51.7 us (98%)
  local copies, waits for them, and re-layouts  0.66 us (1%)
    pallas_call x1, Pallas kernels, layer(): pl.pallas_call(functools.partial(kernel, n), out_shape=pltpu.VMEM((rows,...  51.7 us

profile of v5, /device:TPU:1, one launch (start us, length us, event | category | flops | bytes accessed | tf_op | source)
XLA Modules:
  0.0 52.3 jit_solution(6181441944277660040)
XLA Ops:
  0.0 51.7 %shard_map.64 = bf16[8,8192]{1,0:T(8,128)(2,1)S(1)} custom-call(bf16[8,8192]{1,0:T(8,128)(2,1)} %tok_in.1, f32[1,8192]{1,0:T(1,128)} %bitcast.2, bf16[8192,1024]{1,0:T(8,128)(2,1)} %wg.1, bf16[8192,1024]{1,0:T(8,128)(2,1)} %wu.1, bf16[1024,8192]{1,0:T(8,128)(2,1)} %wd.1, f32[1,1024]{1,0:T(1,128)} %bitcast.3), custom_call_target="tpu_custom_call" | custom-call | tf_op jit(solution)/shard_map/pallas_call | solution.py:433
  51.7 0.7 %copy.8 = bf16[8,8192]{1,0:T(8,128)(2,1)} copy(bf16[8,8192]{1,0:T(8,128)(2,1)S(1)} %shard_map.64) | data formatting | bytes 262144

commit v6 on v5

--- a/solution.py
+++ b/solution.py
@@ -17,7 +17,7 @@
 TURNED = 1
 LAG = ((2, 6), (8, 14), (10, 16), (18, 24))
 TURNED_LAG = ((2, 6), (7, 11), (13, 17), (18, 24))
-LATE = (17, 14)
+LATE = (15, 14)
 MESH = pl.DeviceIdType.MESH
 BF = jnp.bfloat16
 F32 = jnp.float32
@@ -183,6 +183,7 @@
                 relay_line(s, 0, 1)
 
     inner = jnp.logical_not(outer)
+    late = outer & (c == 0)
     for s in range(STEPS + BEHIND + 1):
         if s < STEPS:
             with jax.named_scope(f"relay_line{s}"):
@@ -192,14 +193,17 @@
                         relay_line(s, 0, 1)
                     relay_line(s, 1, line - 1)
                 else:
-                    @pl.when(outer)
+                    @pl.when(late)
                     def _():
                         relay_line(s, 1, line - 1)
         if s == BEHIND:
-            @pl.when(inner)
+            @pl.when(jnp.logical_not(late))
             def _():
                 for later in range(BEHIND + 1, STEPS):
-                    relay_line(later, 0, line - 1)
+                    @pl.when(inner)
+                    def _():
+                        relay_line(later, 0, 1)
+                    relay_line(later, 1, line - 1)
         if 0 <= s - BEHIND < STEPS:
             with jax.named_scope(f"relay_rows{s-BEHIND}"):
                 relay_rows(s - BEHIND)

time: 52.5 us -> 52.6 us (level)
  no operation moved by 1% of the time
where the time goes in v6:
time: 52.6 us; the launch traced here: 52.5 us
  Pallas kernels  51.8 us (98%)
  local copies, waits for them, and re-layouts  0.66 us (1%)
    pallas_call x1, Pallas kernels, layer(): pl.pallas_call(functools.partial(kernel, n), out_shape=pltpu.VMEM((rows,...  51.8 us

profile of v6, /device:TPU:1, one launch (start us, length us, event | category | flops | bytes accessed | tf_op | source)
XLA Modules:
  0.0 52.5 jit_solution(5872145336577353769)
XLA Ops:
  0.0 51.8 %shard_map.64 = bf16[8,8192]{1,0:T(8,128)(2,1)S(1)} custom-call(bf16[8,8192]{1,0:T(8,128)(2,1)} %tok_in.1, f32[1,8192]{1,0:T(1,128)} %bitcast.2, bf16[8192,1024]{1,0:T(8,128)(2,1)} %wg.1, bf16[8192,1024]{1,0:T(8,128)(2,1)} %wu.1, bf16[1024,8192]{1,0:T(8,128)(2,1)} %wd.1, f32[1,1024]{1,0:T(1,128)} %bitcast.3), custom_call_target="tpu_custom_call" | custom-call | tf_op jit(solution)/shard_map/pallas_call | solution.py:437
  51.8 0.7 %copy.8 = bf16[8,8192]{1,0:T(8,128)(2,1)} copy(bf16[8,8192]{1,0:T(8,128)(2,1)S(1)} %shard_map.64) | data formatting | bytes 262144
